TPU v7x, 32 devices: a whole 2x2x4 slice. The times are simulated.
32 devices in a mesh: row: 4 (over y, x), col: 8 (over z, core).
Axes of the slice: x: 2, y: 2, z: 4, core: 2. Of those that a mesh axis runs over, the one named last changes fastest.
Arguments:
- tokens: bfloat16 [512, 16384], P('col', 'row'), may hold values from -6 to 6
- weight: bfloat16 [16384, 32768], P('row', 'col'), may hold values from -0.21875 to 0.21875
- logits: float32 [3, 32768], P(None, 'col'), may hold values from -6 to 303
- cotangent: bfloat16 [512, 32768], P('row', 'col'), may hold values from -6 to 6
Outputs:
- mixed_out: bfloat16 [512, 32768], P('row', 'col')
- input_grad: bfloat16 [512, 16384], P('col', 'row')
- weight_grad: bfloat16 [16384, 32768], P('row', 'col')
- logit_grad: float32 [3, 32768], P(None, 'col')
All inputs are finite; a program needn't handle non-finite values.
Results may differ from a plain program's by a relative error of at most 0.0049.
Values may be sent and summed in bfloat16 or wider, within the bound.
No kernel may reach another device: no remote copies, remote signals or barrier semaphores. Data moves between devices by JAX's collectives and lax.ppermute only.
A program may use at most 192 MiB of HBM per device.

v0:
```python
import math
import jax
import jax.numpy as jnp
from jax import lax
from jax.sharding import PartitionSpec as P

EPSILON = 1e-06
TWO_PI = 2.0 * math.pi
grid_levels = (1.0, 7.0, 127.0)


def quantize(master, peak, scores):
    shares = jax.nn.softmax(scores, axis=0)
    blended = jnp.zeros_like(master)
    slopes = jnp.zeros_like(master)
    candidates = []
    for number, level_value in enumerate(grid_levels):
        spacing = (peak + EPSILON) / level_value
        scaled = master / spacing
        angle_value = TWO_PI * scaled
        candidate = spacing * (scaled - jnp.sin(angle_value) / TWO_PI)
        blended = blended + shares[number] * candidate
        slopes = slopes + shares[number] * (1.0 - jnp.cos(angle_value))
        candidates.append(candidate)
    return (shares, blended, slopes, candidates)


def logit_slopes(shares, terms):
    return shares * (terms - jnp.sum(shares * terms, axis=0, keepdims=True))


def shards(tokens, weight, logits, cotangent):
    master = weight.astype(jnp.float32)
    peak = lax.pmax(jnp.max(jnp.abs(master), axis=0), "row")
    shares, blended, slopes, candidates = quantize(master, peak, logits)
    blend_half = blended.astype(jnp.bfloat16)
    all_cotangent = lax.all_gather(cotangent, "row", axis=0, tiled=True)
    shard_piece = lax.all_gather(tokens, "col", axis=0, tiled=True)
    product = jnp.dot(shard_piece, blend_half, preferred_element_type=jnp.float32)
    outputs_part = product
    outputs_part, all_tokens = (outputs_part, shard_piece)
    mixed_grad = lax.dot_general(
        all_tokens, all_cotangent, (((0,), (0,)), ((), ())), preferred_element_type=jnp.float32
    )
    out_rows = cotangent.shape[0]
    in_rows = tokens.shape[0]
    summed_output = lax.psum(outputs_part, "row")
    outputs_mine = lax.dynamic_slice_in_dim(
        summed_output, lax.axis_index("row") * out_rows, out_rows, 0
    )
    summed_input = lax.psum(
        lax.dot_general(
            all_cotangent, blend_half, (((1,), (1,)), ((), ())), preferred_element_type=jnp.float32
        ),
        "col",
    )
    input_mine = lax.dynamic_slice_in_dim(summed_input, lax.axis_index("col") * in_rows, in_rows, 0)
    mixed_out = outputs_mine.astype(jnp.bfloat16)
    input_grad = input_mine.astype(jnp.bfloat16)
    weight_grad = (mixed_grad * slopes).astype(jnp.bfloat16)
    local_terms = jnp.stack([jnp.sum(mixed_grad * candidate, axis=0) for candidate in candidates])
    terms = lax.psum(local_terms, "row")
    logit_grad = logit_slopes(shares, terms)
    return (mixed_out, input_grad, weight_grad, logit_grad)


def solution(mesh):
    in_specs = (P("col", "row"), P("row", "col"), P(None, "col"), P("row", "col"))
    out_specs = (P("row", "col"), P("col", "row"), P("row", "col"), P(None, "col"))
    return jax.shard_map(shards, mesh=mesh, in_specs=in_specs, out_specs=out_specs, check_vma=False)
```

profile of v0, /device:TPU:0, one launch (start us, length us, event | category | flops | bytes accessed | tf_op | source)
XLA Modules:
  0.0 1547.8 jit_solution(15201740005334068569)
XLA Ops:
  7.2 0.0 copy-start
  7.2 0.0 all-gather.5.cloned.1.call-start
  7.2 0.7 all-gather.5.cloned.1.call-update
  7.9 0.0 all-gather.3.cloned.1.call-start
  8.0 0.7 all-gather.3.cloned.1.call-update
  8.7 0.9 reduce_max.18
  9.6 0.0 copy-start.2
  9.6 11.9 fusion
  21.5 18.4 %pmax.7 = f32[4096]{0:T(1024)S(1)} all-reduce(f32[4096]{0:T(1024)S(1)} %fusion), channel_id=1, replica_groups=mesh['row'=4,'col'=8] {'row'}, use_global_device_ids=true, to_apply=%region_3.0 | all-reduce | flops 4096 | bytes 32768 | tf_op jit(solution)/shard_map/pmax | solution.py:34
  39.9 0.0 copy-done
  39.9 0.1 fusion.2
  39.9 0.0 copy-start.4
  40.0 0.5 copy-done.4
  40.6 24.7 %all-gather.5.cloned.1.call-done = bf16[512,4096]{1,0:T(8,128)(2,1)} async-done(((bf16[128,4096]{1,0:T(8,128)(2,1)}), bf16[512,4096]{1,0:T(8,128)(2,1)}) %all-gather.5.cloned.1.call-update) | async-done | bytes 4194320 | tf_op jit(solution)/shard_map/all_gather | solution.py:37
  65.3 48.5 %all-gather.3.cloned.1.call-done = bf16[512,4096]{1,0:T(8,128)(2,1)} async-done(((bf16[64,4096]{1,0:T(8,128)(2,1)}), bf16[512,4096]{1,0:T(8,128)(2,1)}) %all-gather.3.cloned.1.call-update) | async-done | bytes 4194320 | tf_op jit(solution)/shard_map/all_gather | solution.py:38
  113.8 0.0 copy-start.6
  113.8 917.4 %multiply_reduce_fusion.2 = (f32[4096]{0:T(1024)S(1)}, f32[4096]{0:T(1024)S(1)}, f32[4096]{0:T(1024)S(1)}, bf16[4096,4096]{1,0:T(8,128)(2,1)}, bf16[4096,4096]{1,0:T(8,128)(2,1)}) fusion(f32[4096]{0:T(1024)S(1)} %get-tuple-element.18, bf16[4096,4096]{1,0:T(8,128)(2,1)} %param.5, f32[4096]{0:T(1024)S(1)} %get-tuple-element.20, ...), kind=kOutput, calls=%fused_computation.7 | convolution fusion | flops 17817391104 | bytes 109199360 | tf_op jit(solution)/shard_map/dot_general | solution.py:42
  1031.2 0.0 copy-done.2
  1031.2 0.0 copy-done.6
  1031.2 24.5 %convolution_bitcast_fusion.1 = f32[512,4096]{0,1:T(8,128)} fusion(bf16[4096,4096]{1,0:T(8,128)(2,1)} %get-tuple-element.14, bf16[512,4096]{1,0:T(8,128)(2,1)S(1)} %copy-done.6), kind=kOutput, calls=%fused_computation.14 | convolution fusion | flops 17179869184 | bytes 46137344 | tf_op jit(solution)/shard_map/dot_general | solution.py:39
  1055.8 286.1 %all-reduce.3 = (bf16[512,4096]{0,1:T(8,128)(2,1)}, f32[3,4096]{1,0:T(4,128)S(1)}) all-reduce(f32[512,4096]{0,1:T(8,128)} %convolution_bitcast_fusion.1, f32[3,4096]{1,0:T(4,128)S(1)} %pad_maximum_fusion), channel_id=1, replica_groups=mesh['row'=4,'col'=8] {'row'}, use_global_device_ids=true, to_apply=%region_4.0 | all-reduce | flops 2109440 | bytes 12681216 | tf_op jit(solution)/shard_map/psum | solution.py:47
  1342.0 1.3 dynamic-slice_convert_fusion.1
  1343.3 1.3 copy.8
  1344.6 0.0 copy-start.1
  1344.6 0.0 copy-start.3
  1344.6 0.0 copy-start.5
  1344.6 25.0 %convolution_bitcast_fusion = f32[512,4096]{0,1:T(8,128)} fusion(bf16[4096,4096]{1,0:T(8,128)(2,1)} %get-tuple-element.14, bf16[512,4096]{1,0:T(8,128)(2,1)} %all-gather.5.cloned.1.call-done), kind=kOutput, calls=%fused_computation.13 | convolution fusion | flops 17179869184 | bytes 46137344 | tf_op jit(solution)/shard_map/dot_general | solution.py:52
  1369.6 167.9 %all-reduce.4 = bf16[512,4096]{0,1:T(8,128)(2,1)} all-reduce(f32[512,4096]{0,1:T(8,128)} %convolution_bitcast_fusion), channel_id=1, replica_groups=mesh['row'=4,'col'=8] {'col'}, use_global_device_ids=true, to_apply=%region_5.0 | all-reduce | flops 2097152 | bytes 12582912 | tf_op jit(solution)/shard_map/psum | solution.py:51
  1537.5 1.6 dynamic-slice_convert_fusion
  1539.1 1.1 copy.9
  1540.2 0.0 copy-done.1
  1540.2 0.0 copy-done.3
  1540.2 0.0 copy-done.5
  1540.2 0.1 multiply_reduce_fusion.3
  1540.3 0.7 subtract_multiply_fusion.3
  (4 shorter events, 0.1 us)
Async XLA Ops:
  7.2 32.7 %copy-start = (f32[3,4096]{1,0:T(4,128)S(1)}, f32[3,4096]{1,0:T(4,128)}, u32[]{:S(2)}) copy-start(f32[3,4096]{1,0:T(4,128)} %param.6) | copy-start | bytes 147460
  7.2 58.1 %all-gather.5.cloned.1.call-start = ((), (), s32[]{:S(2)}) async-start(), calls=%async_computation.1 | async-start | bytes 5242880 | tf_op jit(solution)/shard_map/all_gather | solution.py:37
  7.9 105.9 %all-gather.3.cloned.1.call-start = ((), (), s32[]{:S(2)}) async-start(), calls=%async_computation | async-start | bytes 4718592 | tf_op jit(solution)/shard_map/all_gather | solution.py:38
  9.6 1021.7 %copy-start.2 = (f32[4096]{0:T(1024)}, f32[4096]{0:T(1024)S(1)}, u32[]{:S(2)}) copy-start(f32[4096]{0:T(1024)S(1)} %reduce_max.18) | copy-start | bytes 49156
  39.9 0.6 copy-start.4
  113.8 917.5 %copy-start.6 = (bf16[512,4096]{1,0:T(8,128)(2,1)S(1)}, bf16[512,4096]{1,0:T(8,128)(2,1)}, u32[]{:S(2)}) copy-start(bf16[512,4096]{1,0:T(8,128)(2,1)} %all-gather.3.cloned.1.call-done) | copy-start | bytes 12582916
  1344.6 195.7 %copy-start.1 = (f32[3,4096]{1,0:T(4,128)S(1)}, f32[3,4096]{1,0:T(4,128)}, u32[]{:S(2)}) copy-start(f32[3,4096]{1,0:T(4,128)} %param.6) | copy-start | bytes 147460
  1344.6 195.7 %copy-start.3 = (f32[4096]{0:T(1024)S(1)}, f32[4096]{0:T(1024)}, u32[]{:S(2)}) copy-start(f32[4096]{0:T(1024)} %copy-done.2) | copy-start | bytes 49156
  1344.6 195.7 %copy-start.5 = (f32[4096]{0:T(1024)S(1)}, f32[4096]{0:T(1024)}, u32[]{:S(2)}) copy-start(f32[4096]{0:T(1024)} %copy-done.4) | copy-start | bytes 49156
Sparse Core Ops, SparseCore 0:
  9.8 55.4 all-gather.4
  66.9 46.8 all-gather.2
where the time goes:
time: 1550 us
  matrix products  967 us (62%)
  blocking collectives  472 us (30%)
  waiting for transfers between devices  74.6 us (5%)
    dot_general x1, matrix products, shards(): lax.dot_general(all_tokens, all_cotangent, (((0,), (0,)), ((), ())), pref...  917 us
    psum x1, blocking collectives, shards(): summed_output = lax.psum(outputs_part, 'row')  286 us
    psum x1, blocking collectives, shards(): lax.psum(lax.dot_general(all_cotangent, blend_half, (((1,), (1,)), ((), (...  168 us
    all_gather x1, waiting for transfers between devices, shards(): shard_piece = lax.all_gather(tokens, 'col', axis=0, tiled=True)  48.5 us
  transfers between devices with their start and end apart: 2, of which 2 were waited for; matrix products, arithmetic and copies ran while one was open for 1% of the time, Pallas kernels for 0%

commit v1 on v0

--- a/solution.py
+++ b/solution.py
@@ -44,7 +44,11 @@
     )
     out_rows = cotangent.shape[0]
     in_rows = tokens.shape[0]
-    summed_output = lax.psum(outputs_part, "row")
+    summed_output = outputs_part
+    for hop in (1, 2):
+        summed_output = summed_output + lax.ppermute(
+            summed_output, "row", [(dev, dev ^ hop) for dev in range(4)]
+        )
     outputs_mine = lax.dynamic_slice_in_dim(
         summed_output, lax.axis_index("row") * out_rows, out_rows, 0
     )

time: 1550 us -> 2140 us (1.38)
  other arithmetic: 13.7 us -> 790 us
  blocking collectives: 472 us -> 203 us
  waiting for transfers between devices: 74.6 us -> 234 us
  matrix products: 967 us -> 880 us
    convert_element_type x0 -> x2, other arithmetic: none -> 764 us  [the longest x1 761 us: shards(): weight_grad = (mixed_grad * slopes).astype(jnp.bfloat16)]
    psum x1, blocking collectives: 286 us -> 16.9 us  [shards(): terms = lax.psum(local_terms, 'row')]
    ppermute x0 -> x2, waiting for transfers between devices: none -> 160 us  [shards(): lax.ppermute(summed_output, 'row', [(dev, dev ^ hop) for dev in range(4)])]
    dot_general x1, matrix products: 917 us -> 830 us  [shards(): lax.dot_general(all_tokens, all_cotangent, (((0,), (0,)), ((), ())), pref...]
  transfers between devices with their start and end apart: 2 -> 4, of which waited for: 2 -> 4; matrix products, arithmetic and copies ran while one was open for 1% -> 2% of each run, Pallas kernels for 0% -> 0%
where the time goes in v1:
time: 2140 us; the launch traced here: 2130 us
  matrix products  880 us (41%)
  other arithmetic  790 us (37%)
  waiting for transfers between devices  234 us (11%)
  blocking collectives  203 us (9%)
    dot_general x1, matrix products, shards(): lax.dot_general(all_tokens, all_cotangent, (((0,), (0,)), ((), ())), pref...  830 us
    convert_element_type x1, other arithmetic, shards(): weight_grad = (mixed_grad * slopes).astype(jnp.bfloat16)  761 us
    psum x1, blocking collectives, shards(): lax.psum(lax.dot_general(all_cotangent, blend_half, (((1,), (1,)), ((), (...  168 us
    ppermute x2, waiting for transfers between devices, shards(): lax.ppermute(summed_output, 'row', [(dev, dev ^ hop) for dev in range(4)])  160 us
    all_gather x1, waiting for transfers between devices, shards(): shard_piece = lax.all_gather(tokens, 'col', axis=0, tiled=True)  48.5 us
  transfers between devices with their start and end apart: 4, of which 4 were waited for; matrix products, arithmetic and copies ran while one was open for 2% of the time, Pallas kernels for 0%

profile of v1, /device:TPU:0, one launch (start us, length us, event | category | flops | bytes accessed | tf_op | source)
XLA Modules:
  0.0 2126.3 jit_solution(13486704479878830599)
XLA Ops:
  7.2 0.0 all-gather.5.cloned.1.call-start
  7.2 0.7 all-gather.5.cloned.1.call-update
  7.9 0.0 all-gather.3.cloned.1.call-start
  7.9 0.7 all-gather.3.cloned.1.call-update
  8.6 0.9 reduce_max.18
  9.5 0.0 copy-start.1
  9.5 11.9 fusion
  21.5 18.4 pmax.7
  39.8 1.5 fusion.3
  41.4 23.9 %all-gather.5.cloned.1.call-done = bf16[512,4096]{1,0:T(8,128)(2,1)} async-done(((bf16[128,4096]{1,0:T(8,128)(2,1)}), bf16[512,4096]{1,0:T(8,128)(2,1)}) %all-gather.5.cloned.1.call-update) | async-done | bytes 4194320 | tf_op jit(solution)/shard_map/all_gather | solution.py:37
  65.3 48.5 %all-gather.3.cloned.1.call-done = bf16[512,4096]{1,0:T(8,128)(2,1)} async-done(((bf16[64,4096]{1,0:T(8,128)(2,1)}), bf16[512,4096]{1,0:T(8,128)(2,1)}) %all-gather.3.cloned.1.call-update) | async-done | bytes 4194320 | tf_op jit(solution)/shard_map/all_gather | solution.py:38
  113.8 0.0 copy-done.1
  113.8 0.0 copy-start
  113.8 0.0 copy-start.2
  113.8 0.0 copy-start.3
  113.8 830.3 %multiply_reduce_fusion.2 = (f32[4096]{0:T(1024)S(1)}, f32[4096]{0:T(1024)S(1)}, f32[4096]{0:T(1024)S(1)}, f32[4096,4096]{1,0:T(8,128)}) fusion(f32[4096]{0:T(1024)S(1)} %get-tuple-element.20, bf16[4096,4096]{1,0:T(8,128)(2,1)} %param.5, f32[4096]{0:T(1024)S(1)} %get-tuple-element.19, f32[4096]{0:T(1024)S(1)} %get-tuple-element.18, ...), kind=kOutput, calls=%fused_computation.7 | convolution fusion | flops 17548955648 | bytes 109150208 | tf_op jit(solution)/shard_map/dot_general | solution.py:42
  944.1 16.9 psum.15
  961.0 0.0 copy-done
  961.0 0.0 copy-done.2
  961.0 0.0 copy-done.3
  961.0 0.1 multiply_reduce_fusion.3
  961.2 0.0 copy-start.4
  961.2 761.1 %multiply_convert_fusion = (bf16[4096,4096]{1,0:T(8,128)(2,1)}, bf16[4096,4096]{1,0:T(8,128)(2,1)}) fusion(f32[4096,4096]{1,0:T(8,128)} %get-tuple-element.21, f32[4096]{0:T(1024)S(1)} %bitcast.20, f32[4096]{0:T(1024)S(1)} %bitcast.21, f32[4096]{0:T(1024)S(1)} %bitcast.19, f32[4096]{0:T(1024)S(1)} %get-tuple-element.20, bf16[4096,4096]{1,0:T(8,128)(2,1)} %param.5, ...), kind=kLoop, calls=%fused_computation.8 | loop fusion | flops 536870912 | bytes 167870464 | tf_op jit(solution)/shard_map/convert_element_type | solution.py:64
  1722.3 0.0 copy-done.4
  1722.3 24.4 %convolution_bitcast_fusion.1 = f32[512,4096]{0,1:T(8,128)} fusion(bf16[4096,4096]{1,0:T(8,128)(2,1)} %get-tuple-element.14, bf16[512,4096]{1,0:T(8,128)(2,1)S(1)} %copy-done.4), kind=kOutput, calls=%fused_computation.14 | convolution fusion | flops 17179869184 | bytes 46137344 | tf_op jit(solution)/shard_map/dot_general | solution.py:39
  1746.7 0.0 collective-permute-start
  1746.7 25.2 %convolution_bitcast_fusion = f32[512,4096]{0,1:T(8,128)} fusion(bf16[4096,4096]{1,0:T(8,128)(2,1)} %get-tuple-element.14, bf16[512,4096]{1,0:T(8,128)(2,1)} %all-gather.5.cloned.1.call-done), kind=kOutput, calls=%fused_computation.13 | convolution fusion | flops 17179869184 | bytes 46137344 | tf_op jit(solution)/shard_map/dot_general | solution.py:56
  1771.9 153.9 %collective-permute-done = f32[512,4096]{0,1:T(8,128)} collective-permute-done((f32[512,4096]{0,1:T(8,128)}, f32[512,4096]{0,1:T(8,128)}, u32[]{:S(2)}, u32[]{:S(2)}) %collective-permute-start) | collective-permute-done | bytes 8388640 | tf_op jit(solution)/shard_map/ppermute | solution.py:49
  1925.8 11.1 add.36
  1936.9 0.6 collective-permute-start.1
  1937.6 167.9 %all-reduce.1 = bf16[512,4096]{0,1:T(8,128)(2,1)} all-reduce(f32[512,4096]{0,1:T(8,128)} %convolution_bitcast_fusion), channel_id=1, replica_groups=mesh['row'=4,'col'=8] {'col'}, use_global_device_ids=true, to_apply=%region_4.0 | all-reduce | flops 2097152 | bytes 12582912 | tf_op jit(solution)/shard_map/psum | solution.py:55
  2105.5 1.6 dynamic-slice_convert_fusion
  2107.1 1.1 copy.9
  2108.2 0.7 subtract_multiply_fusion.3
  2108.8 6.4 collective-permute-done.1
  2115.2 2.4 fusion.1
  2117.7 1.3 copy.8
  (3 shorter events, 0.1 us)
Async XLA Ops:
  7.2 58.1 %all-gather.5.cloned.1.call-start = ((), (), s32[]{:S(2)}) async-start(), calls=%async_computation.1 | async-start | bytes 5242880 | tf_op jit(solution)/shard_map/all_gather | solution.py:37
  7.9 105.9 %all-gather.3.cloned.1.call-start = ((), (), s32[]{:S(2)}) async-start(), calls=%async_computation | async-start | bytes 4718592 | tf_op jit(solution)/shard_map/all_gather | solution.py:38
  9.5 104.2 %copy-start.1 = (f32[4096]{0:T(1024)}, f32[4096]{0:T(1024)S(1)}, u32[]{:S(2)}) copy-start(f32[4096]{0:T(1024)S(1)} %reduce_max.18) | copy-start | bytes 49156
  113.8 847.2 %copy-start = (f32[3,4096]{1,0:T(4,128)S(1)}, f32[3,4096]{1,0:T(4,128)}, u32[]{:S(2)}) copy-start(f32[3,4096]{1,0:T(4,128)} %param.6) | copy-start | bytes 147460
  113.8 847.2 %copy-start.2 = (f32[4096]{0:T(1024)S(1)}, f32[4096]{0:T(1024)}, u32[]{:S(2)}) copy-start(f32[4096]{0:T(1024)} %copy-done.1) | copy-start | bytes 49156
  113.8 847.3 %copy-start.3 = (f32[4096]{0:T(1024)S(1)}, f32[4096]{0:T(1024)}, u32[]{:S(2)}) copy-start(f32[4096]{0:T(1024)} %fusion.3) | copy-start | bytes 49156
  961.2 761.1 %copy-start.4 = (bf16[512,4096]{1,0:T(8,128)(2,1)S(1)}, bf16[512,4096]{1,0:T(8,128)(2,1)}, u32[]{:S(2)}) copy-start(bf16[512,4096]{1,0:T(8,128)(2,1)} %all-gather.3.cloned.1.call-done) | copy-start | bytes 12582916
  1746.7 179.2 %collective-permute-start = (f32[512,4096]{0,1:T(8,128)}, f32[512,4096]{0,1:T(8,128)}, u32[]{:S(2)}, u32[]{:S(2)}) collective-permute-start(f32[512,4096]{0,1:T(8,128)} %convolution_bitcast_fusion.1), channel_id=1, source_target_pairs={{0,8},{8,0},{16,24},{24,16},{1,9},{9,1},{17,25},{25,17},{2,10},{10... | collective-permute-start | bytes 25165832 | tf_op jit(solution)/shard_map/ppermute | solution.py:49
  1936.9 178.3 %collective-permute-start.1 = (f32[512,4096]{0,1:T(8,128)}, f32[512,4096]{0,1:T(8,128)}, u32[]{:S(2)}, u32[]{:S(2)}) collective-permute-start(f32[512,4096]{0,1:T(8,128)} %add.36), channel_id=1, source_target_pairs={{0,16},{8,24},{16,0},{24,8},{1,17},{9,25},{17,1},{25,9},{2,18},{10... | collective-permute-start | bytes 25165832 | tf_op jit(solution)/shard_map/ppermute | solution.py:49
Sparse Core Ops, SparseCore 0:
  9.8 55.4 all-gather.4
  66.9 46.8 all-gather.2
